TPU v7x, 256 devices: a whole 4x4x8 slice. The times are simulated.
256 devices in a mesh: gx: 8 (over z), gy: 4 (over y_lo, core), gz: 8 (over y_hi, x).
Axes of the slice: x: 4, y: 4 (y_hi: 2, y_lo: 2; y = y_hi * 2 + y_lo), z: 8, core: 2. Of those that a mesh axis runs over, the one named last changes fastest.
Arguments:
- state: bfloat16 [128, 64, 16, 8, 128], P('gx', 'gy', 'gz'), may hold values from -6 to 6
- cotangent: bfloat16 [128, 64, 16, 8, 128], P('gx', 'gy', 'gz'), may hold values from -6 to 6
- counts: int32 [8], P('gz'), may hold values from 1 to 2, 12 in all
- edge_weights: bfloat16 [2, 2, 128, 128], replicated, may hold values from -0.5 to 0.5
- node_in: bfloat16 [2, 256, 128], replicated, may hold values from -0.375 to 0.375
- node_out: bfloat16 [2, 128, 128], replicated, may hold values from -0.5 to 0.5
- biases: float32 [2, 2, 128], replicated, may hold values from -4 to 4
Outputs:
- state_grad: bfloat16 [128, 64, 16, 8, 128], P('gx', 'gy', 'gz')
- edge_grads: float32 [2, 2, 128, 128], replicated
- node_in_grad: float32 [2, 256, 128], replicated
- node_out_grad: float32 [2, 128, 128], replicated
- bias_grads: float32 [2, 2, 128], replicated
Inputs may be any that keep to these rules, and one draw needn't show every extreme that they name: The counts sum to 12; index k of gz holds the element layers that follow those of smaller indices.
All inputs are finite; a program needn't handle non-finite values. No bound on the sum of `counts` on one device may be relied on, other than what follows from the above.
Results may differ from a plain program's by a relative error of at most 0.012.
The roundings to bfloat16 on the way count: a program that leaves them out, or rounds other values in their place, can miss the bound.
Values sent between devices are 32-bit elements; how exact they have to be, the bound alone decides.
A program may use at most 128 MiB of HBM per device.

v0:
```python
import math
import jax
import jax.numpy as jnp
from jax import lax
from jax.sharding import PartitionSpec as P

edge_dims = (1, 3, 5)


def with_halo(cells, sides, width):
    for axis, dim in sides:
        count = lax.axis_size(axis)
        ends = count - 1
        head = lax.slice_in_dim(cells, 0, width, axis=dim)
        tail = lax.slice_in_dim(cells, cells.shape[dim] - width, cells.shape[dim], axis=dim)
        cells = jnp.concatenate(
            [
                lax.ppermute(tail, axis, [(i, (i + 1) % count) for i in range(ends)]),
                cells,
                lax.ppermute(head, axis, [((i + 1) % count, i) for i in range(ends)]),
            ],
            axis=dim,
        )
    return cells


def slice_along(array, start, stop, dim_no):
    return lax.slice_in_dim(array, start, stop, axis=dim_no)


def matmul_rows(left, weight):
    flattened = left.reshape(-1, left.shape[-1])
    product = jnp.dot(flattened, weight, preferred_element_type=jnp.float32)
    return product.reshape(left.shape[:-1] + (weight.shape[-1],))


def cross_rows(left, right):
    return lax.dot_general(
        left.reshape(-1, left.shape[-1]),
        right.reshape(-1, right.shape[-1]),
        (((0,), (0,)), ((), ())),
        preferred_element_type=jnp.float32,
    )


def spread_diff(values, dim_no):
    zero_row = jnp.zeros_like(slice_along(values, 0, 1, dim_no))
    return jnp.concatenate([zero_row, values], dim_no) - jnp.concatenate([values, zero_row], dim_no)


def silu_slope(values):
    sig_value = jax.nn.sigmoid(values)
    return sig_value * (1.0 + values * (1.0 - sig_value))


def edges_forward(features, weight_one, weight_two, bias_edge):
    widened = features.astype(jnp.float32)
    messages = jnp.zeros(features.shape, jnp.float32)
    stored = []
    for dim_no in edge_dims:
        length = features.shape[dim_no]
        differ = (
            slice_along(widened, 1, length, dim_no) - slice_along(widened, 0, length - 1, dim_no)
        ).astype(jnp.bfloat16)
        before = matmul_rows(differ, weight_one) + bias_edge
        active = jax.nn.silu(before).astype(jnp.bfloat16)
        messages = messages + spread_diff(matmul_rows(active, weight_two), dim_no)
        stored.append((differ, before, active))
    return (messages, stored)


def edges_backward(grad_msg, stored, weight_one, weight_two):
    feat_width = grad_msg.shape[-1]
    grad_feat = jnp.zeros(grad_msg.shape, jnp.float32)
    grad_one = jnp.zeros((feat_width, feat_width), jnp.float32)
    grad_two = jnp.zeros((feat_width, feat_width), jnp.float32)
    grad_bias = jnp.zeros((feat_width,), jnp.float32)
    for dim_no, entry in zip(edge_dims, stored):
        differ, before, active = entry
        length = grad_msg.shape[dim_no]
        grad_out = (
            slice_along(grad_msg, 1, length, dim_no) - slice_along(grad_msg, 0, length - 1, dim_no)
        ).astype(jnp.bfloat16)
        grad_two = grad_two + cross_rows(active, grad_out)
        grad_pre = (matmul_rows(grad_out, weight_two.T) * silu_slope(before)).astype(jnp.bfloat16)
        grad_one = grad_one + cross_rows(differ, grad_pre)
        grad_bias = grad_bias + jnp.sum(grad_pre.astype(jnp.float32).reshape(-1, feat_width), 0)
        grad_feat = grad_feat + spread_diff(matmul_rows(grad_pre, weight_one.T), dim_no)
    return (grad_feat, grad_one, grad_two, grad_bias)


def node_forward(features, summed, weight_in, weight_out, bias_node):
    joined = jnp.concatenate([features, summed.astype(jnp.bfloat16)], -1)
    before = matmul_rows(joined, weight_in) + bias_node
    active = jax.nn.silu(before).astype(jnp.bfloat16)
    result = (features.astype(jnp.float32) + matmul_rows(active, weight_out)).astype(jnp.bfloat16)
    return (result, (joined, before, active))


def node_backward(grad_next, stored, weight_in, weight_out):
    joined, before, active = stored
    feat_width = grad_next.shape[-1]
    grad_out_w = cross_rows(active, grad_next)
    grad_pre = (matmul_rows(grad_next, weight_out.T) * silu_slope(before)).astype(jnp.bfloat16)
    grad_in_w = cross_rows(joined, grad_pre)
    grad_bias = jnp.sum(grad_pre.astype(jnp.float32).reshape(-1, feat_width), 0)
    grad_joined = matmul_rows(grad_pre, weight_in.T)
    grad_feat = grad_next.astype(jnp.float32) + grad_joined[..., :feat_width]
    return (grad_feat, grad_joined[..., feat_width:], grad_in_w, grad_out_w, grad_bias)


def couple(array, elem_dim, node_dim):
    moved = jnp.moveaxis(array, (elem_dim, node_dim), (0, 1))
    front_face = moved[:, 0]
    back_face = moved[:, -1]
    zero_face = jnp.zeros_like(front_face[:1])
    new_front = front_face + jnp.concatenate([zero_face, back_face[:-1]], 0)
    new_back = back_face + jnp.concatenate([front_face[1:], zero_face], 0)
    joined = jnp.concatenate([new_front[:, None], moved[:, 1:-1], new_back[:, None]], 1)
    return jnp.moveaxis(joined, (0, 1), (elem_dim, node_dim))


def local_couple(values, dim_no, nodes_edge):
    full_shape = values.shape
    elems_here = full_shape[dim_no] // nodes_edge
    split_shape = full_shape[:dim_no] + (elems_here, nodes_edge) + full_shape[dim_no + 1 :]
    return couple(values.reshape(split_shape), dim_no, dim_no + 1).reshape(full_shape)


def fold_rim(extended, dim_no):
    inner_len = extended.shape[dim_no] - 2
    core_rows = slice_along(extended, 1, inner_len + 1, dim_no)
    front_row = slice_along(core_rows, 0, 1, dim_no) + slice_along(extended, 0, 1, dim_no)
    back_row = slice_along(core_rows, inner_len - 1, inner_len, dim_no) + slice_along(
        extended, inner_len + 1, inner_len + 2, dim_no
    )
    return jnp.concatenate(
        [front_row, slice_along(core_rows, 1, inner_len - 1, dim_no), back_row], dim_no
    )


def on_device(state, cotangent, counts, edge_weights, node_in, node_out, biases):
    nodes_edge = state.shape[3]
    span_x = state.shape[0]
    span_y = state.shape[1]
    elems_x = span_x // nodes_edge
    elems_y = span_y // nodes_edge
    slot_count = state.shape[2]
    grid_shape = state.shape[:4]
    filled = counts[0]
    slot_ids = jnp.arange(slot_count, dtype=jnp.int32)
    node_ids = jnp.arange(nodes_edge, dtype=jnp.int32)
    live_mask = (slot_ids < filled).astype(jnp.float32)[None, None, :, None, None]

    def edge_mult(position, axis_len, elems_here):
        place = jnp.arange(elems_here * nodes_edge, dtype=jnp.int32)
        node_here = place % nodes_edge
        elem_global = position * elems_here + place // nodes_edge
        front_pair = ((node_here == 0) & (elem_global > 0)).astype(jnp.float32)
        back_pair = (
            (node_here == nodes_edge - 1) & (elem_global < elems_here * axis_len - 1)
        ).astype(jnp.float32)
        return 1.0 + front_pair + back_pair

    mult_x = edge_mult(lax.axis_index("gx"), lax.axis_size("gx"), elems_x)
    mult_y = edge_mult(lax.axis_index("gy"), lax.axis_size("gy"), elems_y)
    index_z = lax.axis_index("gz")
    size_z = lax.axis_size("gz")
    lower_mult = ((slot_ids > 0) | (index_z > 0)).astype(jnp.float32)
    upper_mult = ((slot_ids < filled - 1) | (index_z < size_z - 1)).astype(jnp.float32)
    mult_z = (
        1.0
        + (node_ids == 0).astype(jnp.float32)[None, :] * lower_mult[:, None]
        + (node_ids == nodes_edge - 1).astype(jnp.float32)[None, :] * upper_mult[:, None]
    )
    copies = (
        mult_x[:, None, None, None, None]
        * mult_y[None, :, None, None, None]
        * mult_z[None, None, :, :, None]
    )

    def couple_all(values):
        inner = local_couple(local_couple(values, 0, nodes_edge), 1, nodes_edge)
        extended = with_halo(inner, (("gx", 0), ("gy", 1)), 1)
        coupled = fold_rim(fold_rim(extended, 0), 1)
        top_faces = coupled[:, :, :, -1]
        bottom_faces = coupled[:, :, :, 0]
        top_used = lax.dynamic_index_in_dim(top_faces, filled - 1, 2, keepdims=False)
        rim_pair = jnp.stack([bottom_faces[:, :, 0], top_used], 2)
        rim_ext = with_halo(rim_pair, (("gz", 2),), 1)
        from_below = rim_ext[:, :, 0]
        from_above = rim_ext[:, :, 3]
        below_add = jnp.concatenate([from_below[:, :, None], top_faces[:, :, :-1]], 2)
        last_slot = (slot_ids == filled - 1).astype(jnp.float32)[None, None, :, None]
        above_add = (
            jnp.concatenate([bottom_faces[:, :, 1:], jnp.zeros_like(bottom_faces[:, :, :1])], 2)
            + last_slot * from_above[:, :, None]
        )
        result = jnp.concatenate(
            [
                (bottom_faces + below_add)[:, :, :, None],
                coupled[:, :, :, 1:-1],
                (top_faces + above_add)[:, :, :, None],
            ],
            3,
        )
        return result * live_mask

    def to_cells(array):
        return array.reshape(
            (elems_x, nodes_edge, elems_y, nodes_edge, slot_count, nodes_edge, array.shape[-1])
        )

    def to_grid(array):
        return array.reshape(grid_shape + (array.shape[-1],))

    features = state
    grad_next = cotangent * live_mask.astype(jnp.bfloat16)
    saved = []
    for layer_no in range(2):
        messages, edge_store = edges_forward(
            to_cells(features),
            edge_weights[layer_no, 0],
            edge_weights[layer_no, 1],
            biases[layer_no, 0],
        )
        summed = couple_all(to_grid(messages) * live_mask) / copies
        result, node_store = node_forward(
            features, summed, node_in[layer_no], node_out[layer_no], biases[layer_no, 1]
        )
        saved.append((edge_store, node_store))
        features = result
    per_layer = [None, None]
    for layer_no in (1, 0):
        edge_store, node_store = saved[layer_no]
        grad_feat, grad_sum, grad_in_w, grad_out_w, grad_node_b = node_backward(
            grad_next, node_store, node_in[layer_no], node_out[layer_no]
        )
        grad_msg = couple_all(grad_sum / copies * live_mask)
        grad_edge, grad_one, grad_two, grad_edge_b = edges_backward(
            to_cells(grad_msg), edge_store, edge_weights[layer_no, 0], edge_weights[layer_no, 1]
        )
        grad_next = (grad_feat + to_grid(grad_edge)).astype(jnp.bfloat16)
        local_terms = (
            jnp.stack([grad_one, grad_two]),
            grad_in_w,
            grad_out_w,
            jnp.stack([grad_edge_b, grad_node_b]),
        )
        per_layer[layer_no] = local_terms
    stacked = tuple(
        (jnp.stack([per_layer[0][pos_no], per_layer[1][pos_no]]) for pos_no in range(4))
    )
    stacked = lax.psum(stacked, ("gx", "gy", "gz"))
    layers_all = 3 * slot_count * size_z // 4
    nodes_all = (
        nodes_edge**3 * elems_x * lax.axis_size("gx") * elems_y * lax.axis_size("gy") * layers_all
    )
    grad_scale = 1.0 / math.sqrt(nodes_all)
    state_grad = grad_next * live_mask.astype(jnp.bfloat16)
    return (
        state_grad,
        stacked[0] * grad_scale,
        stacked[1] * grad_scale,
        stacked[2] * grad_scale,
        stacked[3] * grad_scale,
    )


def solution(mesh):
    return jax.shard_map(
        on_device,
        mesh=mesh,
        in_specs=(
            P("gx", "gy", "gz", None, None),
            P("gx", "gy", "gz", None, None),
            P("gz"),
            P(),
            P(),
            P(),
            P(),
        ),
        out_specs=(P("gx", "gy", "gz", None, None), P(), P(), P(), P()),
        check_vma=False,
    )
```

profile of v0, /device:TPU:1, one launch (start us, length us, event | category | flops | bytes accessed | tf_op | source)
XLA Modules:
  0.0 601.1 jit_solution(5968325419626531154)
XLA Ops:
  7.2 1.5 convert.3
  9.1 1.4 copy-done
  12.3 1.9 multiply_convert_fusion.14
  15.5 1.8 multiply_convert_fusion.15
  18.3 1.7 fusion.24
  20.0 1.8 multiply_convert_fusion.13
  27.5 4.4 collective-permute-start
  31.8 1.3 collective-permute-start.1
  33.2 2.4 copy_bitcast_fusion.7
  35.6 2.9 collective-permute-done.1
  38.5 1.8 pad_maximum_fusion.49
  40.3 4.7 collective-permute-start.2
  45.0 2.1 collective-permute-start.3
  47.4 4.4 collective-permute-done.3
  51.8 1.5 pad_maximum_fusion
  56.4 3.1 collective-permute-start.4
  59.9 1.5 collective-permute-done.4
  61.6 1.3 collective-permute-start.5
  63.2 4.5 collective-permute-done.5
  68.5 1.7 fusion.13
  70.3 2.1 multiply_convert_fusion.3
  74.4 1.8 multiply_convert_fusion.11
  77.7 1.7 fusion.23
  79.4 1.8 multiply_convert_fusion.10
  86.3 1.4 copy.124
  88.6 3.6 collective-permute-start.6
  92.2 1.3 collective-permute-start.7
  94.8 5.2 collective-permute-done.7
  100.2 4.2 collective-permute-start.8
  104.4 1.9 collective-permute-start.9
  106.5 4.4 collective-permute-done.9
  112.7 3.6 collective-permute-start.10
  116.4 1.9 collective-permute-done.10
  119.0 1.3 collective-permute-start.11
  121.6 3.5 collective-permute-done.11
  127.8 1.3 convert_reduce_fusion
  133.8 4.6 collective-permute-start.12
  138.4 1.3 collective-permute-start.13
  140.9 4.1 collective-permute-done.13
  145.3 4.2 collective-permute-start.14
  149.5 1.9 collective-permute-start.15
  152.4 3.6 collective-permute-done.15
  157.7 5.7 collective-permute-start.16
  165.5 1.5 collective-permute-start.17
  168.5 3.4 collective-permute-done.17
  192.4 3.6 collective-permute-start.18
  199.0 3.5 collective-permute-done.19
  202.7 4.2 collective-permute-start.20
  206.9 1.9 collective-permute-start.21
  209.5 3.8 collective-permute-done.21
  215.2 7.3 %collective-permute-start.22 = (f32[16,16,1,128]{3,1,0,2:T(8,128)S(1)}, f32[16,16,1,128]{3,1,0,2:T(8,128)S(1)}, u32[]{:S(2)}, u32[]{:S(2)}) collective-permute-start(f32[16,16,1,128]{3,1,0,2:T(8,128)S(1)} %dynamic-slice_bitcast_fusion), channel_id=1, source_target_pairs={{0,1},{1,2},{2,3},{3,4},{4,5},{5,6},{6,7},{8,9},{9,10},{10,11},{11... | collective-permute-start | bytes 393224 | tf_op jit(solution)/shard_map/ppermute | solution.py:18
  224.5 1.5 collective-permute-start.23
  227.5 3.4 collective-permute-done.23
  237.5 1.7 fusion.129
  244.4 1.8 convert_reduce_fusion.7
  246.3 84.3 %psum.31 = f32[2,2,128]{2,1,0:T(2,128)S(1)} all-reduce(f32[2,2,128]{2,1,0:T(2,128)S(1)} %pad_maximum_fusion.51), channel_id=1, replica_groups=mesh['gx'=8,'gy'=4,'gz'=8] {'gx','gy','gz'}, use_global_device_ids=true, to_apply=%region_11.12 | all-reduce | flops 512 | bytes 4096 | tf_op jit(solution)/shard_map/psum | solution.py:254
  331.2 2.8 fusion.131
  334.0 1.4 fusion.36
  336.7 4.3 subtract_add_fusion
  341.1 1.5 fusion.43
  342.6 246.3 %all-reduce.47.cloned.1.call-done = (f32[2,2,128,128]{3,2,1,0:T(8,128)}, f32[2,256,128]{2,1,0:T(8,128)}, f32[2,128,128]{2,1,0:T(8,128)}) async-done(((f32[2,2,128,128]{3,2,1,0:T(8,128)}, f32[2,256,128]{2,1,0:T(8,128)}, f32[2,128,128]{2,1,0:T(8,128)}), (f32[2,2,128,128]{3,2,1,0:T(8,128)}, f32[2,256,128]{2,1,0:T(8,128)}, f32[2,128,128]{2,1,0:T(8,128)})) %all-reduce.47.cloned.1.call-update) | async-done | bytes 655376 | tf_op jit(solution)/shard_map/psum | solution.py:254
  588.9 1.7 broadcast_multiply_fusion.3
  590.5 1.6 broadcast_multiply_fusion.5
  592.1 1.7 broadcast_multiply_fusion.2
  (300 shorter events, 86.8 us)
Async XLA Ops:
  7.2 581.7 %all-reduce.47.cloned.1.call-start = ((), (), s32[]{:S(2)}) async-start(), calls=%async_computation | async-start | bytes 1310720 | tf_op jit(solution)/shard_map/psum | solution.py:254
  8.9 6.6 %copy-start.14 = (bf16[2,7,2,8,2,8,128]{6,5,4,3,2,1,0:T(8,128)(2,1)}, bf16[2,7,2,8,2,8,128]{6,5,4,3,2,1,0:T(8,128)(2,1)S(1)}, u32[]{:S(2)}) copy-start(bf16[2,7,2,8,2,8,128]{6,5,4,3,2,1,0:T(8,128)(2,1)S(1)} %fusion.22) | copy-start | bytes 2752516
  8.9 1.6 copy-start
  10.5 1.8 copy-start.18
  10.5 1.2 copy-start.27
  10.5 1.8 copy-start.9
  12.3 7.7 %copy-start.28 = (f32[128]{0:T(128)}, f32[128]{0:T(128)S(1)}, u32[]{:S(2)}) copy-start(f32[128]{0:T(128)S(1)} %get-tuple-element.80) | copy-start | bytes 1540
  14.2 0.9 copy-start.20
  17.4 0.9 copy-start.16
  20.0 1.8 copy-start.12
  21.8 1.2 copy-start.7
  25.4 1.3 copy-start.1
  25.7 7.5 %copy-start.4 = (f32[2,16,2,8,128]{4,0,3,2,1:T(2,128)}, f32[2,16,2,8,128]{4,0,3,2,1:T(2,128)S(1)}, u32[]{:S(2)}) copy-start(f32[2,16,2,8,128]{4,0,3,2,1:T(2,128)S(1)} %copy_add_fusion.4) | copy-start | bytes 786436
  27.5 8.1 %collective-permute-start = (f32[1,16,2,8,128]{4,1,0,3,2:T(8,128)}, f32[1,16,2,8,128]{4,1,0,3,2:T(8,128)S(1)}, u32[]{:S(2)}, u32[]{:S(2)}) collective-permute-start(f32[1,16,2,8,128]{4,1,0,3,2:T(8,128)} %get-tuple-element.56), channel_id=1, source_target_pairs={{0,32},{32,64},{64,96},{96,128},{128,160},{160,192},{192,224},{1,3... | collective-permute-start | bytes 393224 | tf_op jit(solution)/shard_map/ppermute | solution.py:18
  31.8 6.7 %collective-permute-start.1 = (f32[1,16,2,8,128]{4,1,0,3,2:T(8,128)}, f32[1,16,2,8,128]{4,1,0,3,2:T(8,128)}, u32[]{:S(2)}, u32[]{:S(2)}) collective-permute-start(f32[1,16,2,8,128]{4,1,0,3,2:T(8,128)} %get-tuple-element.57), channel_id=1, source_target_pairs={{32,0},{64,32},{96,64},{128,96},{160,128},{192,160},{224,192},{33,... | collective-permute-start | bytes 393224 | tf_op jit(solution)/shard_map/ppermute | solution.py:20
  40.3 7.1 %collective-permute-start.2 = (f32[18,1,2,8,128]{4,1,0,3,2:T(1,128)}, f32[18,1,2,8,128]{4,1,0,3,2:T(1,128)S(1)}, u32[]{:S(2)}, u32[]{:S(2)}) collective-permute-start(f32[18,1,2,8,128]{4,1,0,3,2:T(1,128)} %get-tuple-element.30), channel_id=1, source_target_pairs={{0,8},{8,16},{16,24},{1,9},{9,17},{17,25},{2,10},{10,18},{18,26},{... | collective-permute-start | bytes 442376 | tf_op jit(solution)/shard_map/ppermute | solution.py:18
  45.0 6.8 %collective-permute-start.3 = (f32[18,1,2,8,128]{4,1,0,3,2:T(1,128)}, f32[18,1,2,8,128]{4,1,0,3,2:T(1,128)}, u32[]{:S(2)}, u32[]{:S(2)}) collective-permute-start(f32[18,1,2,8,128]{4,1,0,3,2:T(1,128)} %get-tuple-element.31), channel_id=1, source_target_pairs={{8,0},{16,8},{24,16},{9,1},{17,9},{25,17},{10,2},{18,10},{26,18},{... | collective-permute-start | bytes 442376 | tf_op jit(solution)/shard_map/ppermute | solution.py:20
  47.4 5.9 copy-start.5
  53.5 1.0 copy-start.6
  56.4 5.1 collective-permute-start.4
  61.6 6.1 %collective-permute-start.5 = (f32[16,16,1,128]{3,1,0,2:T(8,128)S(1)}, f32[16,16,1,128]{3,1,0,2:T(8,128)S(1)}, u32[]{:S(2)}, u32[]{:S(2)}) collective-permute-start(f32[16,16,1,128]{3,1,0,2:T(8,128)S(1)} %get-tuple-element.76), channel_id=1, source_target_pairs={{1,0},{2,1},{3,2},{4,3},{5,4},{6,5},{7,6},{9,8},{10,9},{11,10},{12... | collective-permute-start | bytes 393224 | tf_op jit(solution)/shard_map/ppermute | solution.py:20
  68.5 1.8 copy-start.25
  68.5 1.8 copy-start.30
  70.3 2.1 copy-start.26
  73.5 0.9 copy-start.10
  88.6 6.2 %collective-permute-start.6 = (f32[1,16,2,8,128]{4,1,0,2,3:T(8,128)S(1)}, f32[1,16,2,8,128]{4,1,0,2,3:T(8,128)S(1)}, u32[]{:S(2)}, u32[]{:S(2)}) collective-permute-start(f32[1,16,2,8,128]{4,1,0,2,3:T(8,128)S(1)} %get-tuple-element.48), channel_id=1, source_target_pairs={{0,32},{32,64},{64,96},{96,128},{128,160},{160,192},{192,224},{1,3... | collective-permute-start | bytes 393224 | tf_op jit(solution)/shard_map/ppermute | solution.py:18
  92.2 7.8 %collective-permute-start.7 = (f32[1,16,2,8,128]{4,1,0,2,3:T(8,128)S(1)}, f32[1,16,2,8,128]{4,1,0,2,3:T(8,128)S(1)}, u32[]{:S(2)}, u32[]{:S(2)}) collective-permute-start(f32[1,16,2,8,128]{4,1,0,2,3:T(8,128)S(1)} %get-tuple-element.49), channel_id=1, source_target_pairs={{32,0},{64,32},{96,64},{128,96},{160,128},{192,160},{224,192},{33,... | collective-permute-start | bytes 393224 | tf_op jit(solution)/shard_map/ppermute | solution.py:20
  100.2 6.3 %collective-permute-start.8 = (f32[18,1,2,8,128]{4,1,0,2,3:T(1,128)S(1)}, f32[18,1,2,8,128]{4,1,0,2,3:T(1,128)S(1)}, u32[]{:S(2)}, u32[]{:S(2)}) collective-permute-start(f32[18,1,2,8,128]{4,1,0,2,3:T(1,128)S(1)} %get-tuple-element.28), channel_id=1, source_target_pairs={{0,8},{8,16},{16,24},{1,9},{9,17},{17,25},{2,10},{10,18},{18,26},{... | collective-permute-start | bytes 442376 | tf_op jit(solution)/shard_map/ppermute | solution.py:18
  104.4 6.5 %collective-permute-start.9 = (f32[18,1,2,8,128]{4,1,0,2,3:T(1,128)S(1)}, f32[18,1,2,8,128]{4,1,0,2,3:T(1,128)S(1)}, u32[]{:S(2)}, u32[]{:S(2)}) collective-permute-start(f32[18,1,2,8,128]{4,1,0,2,3:T(1,128)S(1)} %get-tuple-element.29), channel_id=1, source_target_pairs={{8,0},{16,8},{24,16},{9,1},{17,9},{25,17},{10,2},{18,10},{26,18},{... | collective-permute-start | bytes 442376 | tf_op jit(solution)/shard_map/ppermute | solution.py:20
  112.7 5.6 collective-permute-start.10
  119.0 6.1 %collective-permute-start.11 = (f32[16,16,1,128]{3,2,1,0:T(1,128)S(1)}, f32[16,16,1,128]{3,2,1,0:T(1,128)S(1)}, u32[]{:S(2)}, u32[]{:S(2)}) collective-permute-start(f32[16,16,1,128]{3,2,1,0:T(1,128)S(1)} %get-tuple-element.74), channel_id=1, source_target_pairs={{1,0},{2,1},{3,2},{4,3},{5,4},{6,5},{7,6},{9,8},{10,9},{11,10},{12... | collective-permute-start | bytes 393224 | tf_op jit(solution)/shard_map/ppermute | solution.py:20
  126.6 1.2 copy-start.11
  126.6 1.2 copy-start.32
  133.8 7.2 %collective-permute-start.12 = (f32[1,16,2,8,128]{4,1,0,3,2:T(8,128)S(1)}, f32[1,16,2,8,128]{4,1,0,3,2:T(8,128)S(1)}, u32[]{:S(2)}, u32[]{:S(2)}) collective-permute-start(f32[1,16,2,8,128]{4,1,0,3,2:T(8,128)S(1)} %get-tuple-element.40), channel_id=1, source_target_pairs={{0,32},{32,64},{64,96},{96,128},{128,160},{160,192},{192,224},{1,3... | collective-permute-start | bytes 393224 | tf_op jit(solution)/shard_map/ppermute | solution.py:18
  138.4 6.7 %collective-permute-start.13 = (f32[1,16,2,8,128]{4,1,0,3,2:T(8,128)S(1)}, f32[1,16,2,8,128]{4,1,0,3,2:T(8,128)S(1)}, u32[]{:S(2)}, u32[]{:S(2)}) collective-permute-start(f32[1,16,2,8,128]{4,1,0,3,2:T(8,128)S(1)} %get-tuple-element.41), channel_id=1, source_target_pairs={{32,0},{64,32},{96,64},{128,96},{160,128},{192,160},{224,192},{33,... | collective-permute-start | bytes 393224 | tf_op jit(solution)/shard_map/ppermute | solution.py:20
  145.3 7.1 %collective-permute-start.14 = (f32[18,1,2,8,128]{4,1,0,3,2:T(1,128)S(1)}, f32[18,1,2,8,128]{4,1,0,3,2:T(1,128)S(1)}, u32[]{:S(2)}, u32[]{:S(2)}) collective-permute-start(f32[18,1,2,8,128]{4,1,0,3,2:T(1,128)S(1)} %get-tuple-element.24), channel_id=1, source_target_pairs={{0,8},{8,16},{16,24},{1,9},{9,17},{17,25},{2,10},{10,18},{18,26},{... | collective-permute-start | bytes 442376 | tf_op jit(solution)/shard_map/ppermute | solution.py:18
  149.5 6.5 %collective-permute-start.15 = (f32[18,1,2,8,128]{4,1,0,3,2:T(1,128)S(1)}, f32[18,1,2,8,128]{4,1,0,3,2:T(1,128)S(1)}, u32[]{:S(2)}, u32[]{:S(2)}) collective-permute-start(f32[18,1,2,8,128]{4,1,0,3,2:T(1,128)S(1)} %get-tuple-element.25), channel_id=1, source_target_pairs={{8,0},{16,8},{24,16},{9,1},{17,9},{25,17},{10,2},{18,10},{26,18},{... | collective-permute-start | bytes 442376 | tf_op jit(solution)/shard_map/ppermute | solution.py:20
  157.7 7.6 %collective-permute-start.16 = (f32[16,16,1,128]{3,1,0,2:T(8,128)S(1)}, f32[16,16,1,128]{3,1,0,2:T(8,128)S(1)}, u32[]{:S(2)}, u32[]{:S(2)}) collective-permute-start(f32[16,16,1,128]{3,1,0,2:T(8,128)S(1)} %dynamic-slice_bitcast_fusion.1), channel_id=1, source_target_pairs={{0,1},{1,2},{2,3},{3,4},{4,5},{5,6},{6,7},{8,9},{9,10},{10,11},{11... | collective-permute-start | bytes 393224 | tf_op jit(solution)/shard_map/ppermute | solution.py:18
  165.5 6.4 %collective-permute-start.17 = (f32[16,16,1,128]{3,1,0,2:T(8,128)S(1)}, f32[16,16,1,128]{3,1,0,2:T(8,128)S(1)}, u32[]{:S(2)}, u32[]{:S(2)}) collective-permute-start(f32[16,16,1,128]{3,1,0,2:T(8,128)S(1)} %get-tuple-element.70), channel_id=1, source_target_pairs={{1,0},{2,1},{3,2},{4,3},{5,4},{6,5},{7,6},{9,8},{10,9},{11,10},{12... | collective-permute-start | bytes 393224 | tf_op jit(solution)/shard_map/ppermute | solution.py:20
  173.7 1.5 copy-start.36
  177.0 1.5 copy-start.37
  182.8 1.6 copy-start.38
  187.3 2.0 copy-start.2
  192.4 6.6 %collective-permute-start.18 = (f32[1,16,2,8,128]{4,1,0,3,2:T(8,128)S(1)}, f32[1,16,2,8,128]{4,1,0,3,2:T(8,128)S(1)}, u32[]{:S(2)}, u32[]{:S(2)}) collective-permute-start(f32[1,16,2,8,128]{4,1,0,3,2:T(8,128)S(1)} %get-tuple-element.32), channel_id=1, source_target_pairs={{0,32},{32,64},{64,96},{96,128},{128,160},{160,192},{192,224},{1,3... | collective-permute-start | bytes 393224 | tf_op jit(solution)/shard_map/ppermute | solution.py:18
  196.1 6.4 %collective-permute-start.19 = (f32[1,16,2,8,128]{4,1,0,3,2:T(8,128)S(1)}, f32[1,16,2,8,128]{4,1,0,3,2:T(8,128)S(1)}, u32[]{:S(2)}, u32[]{:S(2)}) collective-permute-start(f32[1,16,2,8,128]{4,1,0,3,2:T(8,128)S(1)} %get-tuple-element.33), channel_id=1, source_target_pairs={{32,0},{64,32},{96,64},{128,96},{160,128},{192,160},{224,192},{33,... | collective-permute-start | bytes 393224 | tf_op jit(solution)/shard_map/ppermute | solution.py:20
  202.7 6.9 %collective-permute-start.20 = (f32[18,1,2,8,128]{4,1,0,3,2:T(1,128)S(1)}, f32[18,1,2,8,128]{4,1,0,3,2:T(1,128)S(1)}, u32[]{:S(2)}, u32[]{:S(2)}) collective-permute-start(f32[18,1,2,8,128]{4,1,0,3,2:T(1,128)S(1)} %get-tuple-element.22), channel_id=1, source_target_pairs={{0,8},{8,16},{16,24},{1,9},{9,17},{17,25},{2,10},{10,18},{18,26},{... | collective-permute-start | bytes 442376 | tf_op jit(solution)/shard_map/ppermute | solution.py:18
  206.9 6.5 %collective-permute-start.21 = (f32[18,1,2,8,128]{4,1,0,3,2:T(1,128)S(1)}, f32[18,1,2,8,128]{4,1,0,3,2:T(1,128)S(1)}, u32[]{:S(2)}, u32[]{:S(2)}) collective-permute-start(f32[18,1,2,8,128]{4,1,0,3,2:T(1,128)S(1)} %get-tuple-element.23), channel_id=1, source_target_pairs={{8,0},{16,8},{24,16},{9,1},{17,9},{25,17},{10,2},{18,10},{26,18},{... | collective-permute-start | bytes 442376 | tf_op jit(solution)/shard_map/ppermute | solution.py:20
  215.2 9.2 %collective-permute-start.22 = (f32[16,16,1,128]{3,1,0,2:T(8,128)S(1)}, f32[16,16,1,128]{3,1,0,2:T(8,128)S(1)}, u32[]{:S(2)}, u32[]{:S(2)}) collective-permute-start(f32[16,16,1,128]{3,1,0,2:T(8,128)S(1)} %dynamic-slice_bitcast_fusion), channel_id=1, source_target_pairs={{0,1},{1,2},{2,3},{3,4},{4,5},{5,6},{6,7},{8,9},{9,10},{10,11},{11... | collective-permute-start | bytes 393224 | tf_op jit(solution)/shard_map/ppermute | solution.py:18
  224.5 6.4 %collective-permute-start.23 = (f32[16,16,1,128]{3,1,0,2:T(8,128)S(1)}, f32[16,16,1,128]{3,1,0,2:T(8,128)S(1)}, u32[]{:S(2)}, u32[]{:S(2)}) collective-permute-start(f32[16,16,1,128]{3,1,0,2:T(8,128)S(1)} %get-tuple-element.68), channel_id=1, source_target_pairs={{1,0},{2,1},{3,2},{4,3},{5,4},{6,5},{7,6},{9,8},{10,9},{11,10},{12... | collective-permute-start | bytes 393224 | tf_op jit(solution)/shard_map/ppermute | solution.py:20
  232.2 11.2 %copy-start.22 = (bf16[2,7,2,8,2,8,128]{6,5,4,3,2,1,0:T(8,128)(2,1)}, bf16[2,7,2,8,2,8,128]{6,5,4,3,2,1,0:T(8,128)(2,1)S(1)}, u32[]{:S(2)}) copy-start(bf16[2,7,2,8,2,8,128]{6,5,4,3,2,1,0:T(8,128)(2,1)S(1)} %fusion.16) | copy-start | bytes 2752516
  232.4 1.3 copy-start.21
  233.7 1.5 copy-start.34
  235.2 1.2 copy-start.19
  237.5 1.7 copy-start.8
  239.2 1.5 copy-start.35
  240.7 1.2 copy-start.13
  242.9 1.5 copy-start.33
  330.6 3.4 copy-start.17
  330.6 3.4 copy-start.23
  334.0 1.5 copy-start.15
  334.0 1.5 copy-start.24
  334.0 1.5 copy-start.39
  334.0 1.5 copy-start.40
  336.7 4.4 copy-start.3
  (2 other events, 1.6 us)
Sparse Core Ops, SparseCore 0:
  336.8 251.9 all-reduce.46
where the time goes:
time: 610 us; the launch traced here: 601 us
  waiting for transfers between devices  300 us (49%)
  blocking collectives  84.3 us (14%)
  starting transfers between devices  71.9 us (12%)
  other arithmetic  53.6 us (9%)
  matrix products  43.4 us (7%)
  local copies, waits for them, and re-layouts  31.1 us (5%)
  between operations  17 us (3%)
    psum x1, waiting for transfers between devices, on_device(): stacked = lax.psum(stacked, ('gx', 'gy', 'gz'))  246 us
    psum x1, blocking collectives, on_device(): stacked = lax.psum(stacked, ('gx', 'gy', 'gz'))  84.3 us
    ppermute x12, starting transfers between devices, with_halo(): lax.ppermute(tail, axis, [(i, (i + 1) % count) for i in range(ends)])  53.2 us
    ppermute x12, waiting for transfers between devices, with_halo(): lax.ppermute(head, axis, [((i + 1) % count, i) for i in range(ends)])  46.7 us
    dot_general x31, matrix products, matmul_rows(): product = jnp.dot(flattened, weight, preferred_element_type=jnp.float32)  31.6 us
    ppermute x12, starting transfers between devices, with_halo(): lax.ppermute(head, axis, [((i + 1) % count, i) for i in range(ends)])  18.6 us
    unnamed x82, local copies, waits for them, and re-layouts  12.7 us
  transfers between devices with their start and end apart: 25, of which 21 were waited for; matrix products, arithmetic and copies ran while one was open for 3% of the time, Pallas kernels for 0%

commit v1 on v0

--- a/solution.py
+++ b/solution.py
@@ -251,7 +251,7 @@
     stacked = tuple(
         (jnp.stack([per_layer[0][pos_no], per_layer[1][pos_no]]) for pos_no in range(4))
     )
-    stacked = lax.psum(stacked, ("gx", "gy", "gz"))
+    stacked = lax.psum(lax.psum(stacked, "gx"), ("gy", "gz"))
     layers_all = 3 * slot_count * size_z // 4
     nodes_all = (
         nodes_edge**3 * elems_x * lax.axis_size("gx") * elems_y * lax.axis_size("gy") * layers_all

time: 610 us -> 554 us (0.908)
  waiting for transfers between devices: 300 us -> 239 us
  blocking collectives: 84.3 us -> 94 us
  matrix products: 43.4 us -> 36.1 us
    psum x1 -> x2, waiting for transfers between devices: 246 us -> 185 us  [on_device(): stacked = lax.psum(lax.psum(stacked, 'gx'), ('gy', 'gz'))]
    psum x1 -> x2, blocking collectives: 84.3 us -> 94 us  [on_device(): stacked = lax.psum(lax.psum(stacked, 'gx'), ('gy', 'gz'))]
    unnamed x82 -> x78, local copies, waits for them, and re-layouts: 12.7 us -> 13.7 us
  transfers between devices with their start and end apart: 25 -> 26, of which waited for: 21 -> 22; matrix products, arithmetic and copies ran while one was open for 3% -> 4% of each run, Pallas kernels for 0% -> 0%
where the time goes in v1:
time: 554 us; the launch traced here: 545 us
  waiting for transfers between devices  239 us (43%)
  blocking collectives  94 us (17%)
  starting transfers between devices  71.9 us (13%)
  other arithmetic  55.5 us (10%)
  matrix products  36.1 us (7%)
  local copies, waits for them, and re-layouts  32.1 us (6%)
  between operations  17 us (3%)
    psum x2, waiting for transfers between devices, on_device(): stacked = lax.psum(lax.psum(stacked, 'gx'), ('gy', 'gz'))  185 us
    psum x2, blocking collectives, on_device(): stacked = lax.psum(lax.psum(stacked, 'gx'), ('gy', 'gz'))  94 us
    ppermute x12, starting transfers between devices, with_halo(): lax.ppermute(tail, axis, [(i, (i + 1) % count) for i in range(ends)])  53.2 us
    ppermute x12, waiting for transfers between devices, with_halo(): lax.ppermute(head, axis, [((i + 1) % count, i) for i in range(ends)])  46.7 us
    dot_general x31, matrix products, matmul_rows(): product = jnp.dot(flattened, weight, preferred_element_type=jnp.float32)  27.2 us
    ppermute x12, starting transfers between devices, with_halo(): lax.ppermute(head, axis, [((i + 1) % count, i) for i in range(ends)])  18.6 us
    unnamed x78, local copies, waits for them, and re-layouts  13.7 us
  transfers between devices with their start and end apart: 26, of which 22 were waited for; matrix products, arithmetic and copies ran while one was open for 4% of the time, Pallas kernels for 0%

profile of v1, /device:TPU:1, one launch (start us, length us, event | category | flops | bytes accessed | tf_op | source)
XLA Modules:
  0.0 545.1 jit_solution(2615638030302375779)
XLA Ops:
  7.2 1.5 convert.3
  9.1 1.4 copy-done
  12.3 1.9 multiply_convert_fusion.14
  15.5 1.8 multiply_convert_fusion.15
  18.3 1.7 fusion.24
  20.0 1.8 multiply_convert_fusion.13
  28.5 4.4 collective-permute-start
  32.9 1.3 collective-permute-start.1
  34.3 2.4 copy_bitcast_fusion.7
  36.7 2.9 collective-permute-done.1
  39.6 1.8 pad_maximum_fusion.49
  41.3 4.7 collective-permute-start.2
  46.1 2.1 collective-permute-start.3
  48.5 4.4 collective-permute-done.3
  52.8 1.5 pad_maximum_fusion
  57.5 3.1 collective-permute-start.4
  61.0 1.5 collective-permute-done.4
  62.6 1.3 collective-permute-start.5
  64.3 4.5 collective-permute-done.5
  69.7 1.7 fusion.13
  71.4 2.1 multiply_convert_fusion.3
  77.6 1.7 fusion.23
  85.0 1.4 copy.124
  87.4 3.5 collective-permute-start.6
  90.9 1.3 collective-permute-start.7
  93.5 5.2 collective-permute-done.7
  99.0 4.2 collective-permute-start.8
  103.2 1.9 collective-permute-start.9
  105.3 4.4 collective-permute-done.9
  111.5 3.6 collective-permute-start.10
  115.2 1.9 collective-permute-done.10
  117.8 1.3 collective-permute-start.11
  120.4 3.5 collective-permute-done.11
  126.6 1.3 convert_reduce_fusion
  132.5 4.6 collective-permute-start.12
  137.1 1.3 collective-permute-start.13
  139.7 4.1 collective-permute-done.13
  144.0 4.2 collective-permute-start.14
  148.3 1.9 collective-permute-start.15
  151.2 3.6 collective-permute-done.15
  156.5 5.7 %collective-permute-start.16 = (f32[16,16,1,128]{3,1,0,2:T(8,128)S(1)}, f32[16,16,1,128]{3,1,0,2:T(8,128)S(1)}, u32[]{:S(2)}, u32[]{:S(2)}) collective-permute-start(f32[16,16,1,128]{3,1,0,2:T(8,128)S(1)} %dynamic-slice_bitcast_fusion.1), channel_id=1, source_target_pairs={{0,1},{1,2},{2,3},{3,4},{4,5},{5,6},{6,7},{8,9},{9,10},{10,11},{11... | collective-permute-start | bytes 393224 | tf_op jit(solution)/shard_map/ppermute | solution.py:18
  164.2 1.5 collective-permute-start.17
  167.2 3.4 collective-permute-done.17
  185.1 1.2 copy-done.2
  189.5 3.6 collective-permute-start.18
  193.1 1.3 collective-permute-start.19
  196.0 3.5 collective-permute-done.19
  199.7 4.2 collective-permute-start.20
  204.0 1.9 collective-permute-start.21
  206.6 3.8 collective-permute-done.21
  212.3 7.2 %collective-permute-start.22 = (f32[16,16,1,128]{3,1,0,2:T(8,128)S(1)}, f32[16,16,1,128]{3,1,0,2:T(8,128)S(1)}, u32[]{:S(2)}, u32[]{:S(2)}) collective-permute-start(f32[16,16,1,128]{3,1,0,2:T(8,128)S(1)} %dynamic-slice_bitcast_fusion), channel_id=1, source_target_pairs={{0,1},{1,2},{2,3},{3,4},{4,5},{5,6},{6,7},{8,9},{9,10},{10,11},{11... | collective-permute-start | bytes 393224 | tf_op jit(solution)/shard_map/ppermute | solution.py:18
  221.6 1.5 collective-permute-start.23
  224.6 3.4 collective-permute-done.23
  234.0 1.7 fusion.44
  240.9 11.9 %psum.62 = f32[2,2,128]{2,1,0:T(2,128)S(1)} all-reduce(f32[2,2,128]{2,1,0:T(2,128)S(1)} %pad_maximum_fusion.51), channel_id=1, replica_groups=mesh['gx'=8,'gy'=4,'gz'=8] {'gx'}, use_global_device_ids=true, to_apply=%region_14.15 | all-reduce | flops 512 | bytes 4096 | tf_op jit(solution)/shard_map/psum | solution.py:254
  252.8 82.1 %psum.63 = f32[2,2,128]{2,1,0:T(2,128)S(1)} all-reduce(f32[2,2,128]{2,1,0:T(2,128)S(1)} %psum.62), channel_id=1, replica_groups=mesh['gx'=8,'gy'=4,'gz'=8] {'gy','gz'}, use_global_device_ids=true, to_apply=%region_15.16 | all-reduce | flops 512 | bytes 4096 | tf_op jit(solution)/shard_map/psum | solution.py:254
  334.8 1.7 fusion.131
  339.7 4.4 subtract_add_fusion
  344.7 67.7 %all-reduce.51.cloned.1.call-done = (f32[2,2,128,128]{3,2,1,0:T(8,128)}, f32[2,256,128]{2,1,0:T(8,128)}, f32[2,128,128]{2,1,0:T(8,128)}) async-done(((f32[2,2,128,128]{3,2,1,0:T(8,128)}, f32[2,256,128]{2,1,0:T(8,128)}, f32[2,128,128]{2,1,0:T(8,128)}), (f32[2,2,128,128]{3,2,1,0:T(8,128)}, f32[2,256,128]{2,1,0:T(8,128)}, f32[2,128,128]{2,1,0:T(8,128)})) %all-reduce.51.cloned.1.call-update) | async-done | bytes 655376 | tf_op jit(solution)/shard_map/psum | solution.py:254
  412.5 3.0 fusion.43
  415.5 117.4 %all-reduce.49.cloned.1.call-done = (f32[2,2,128,128]{3,2,1,0:T(8,128)}, f32[2,256,128]{2,1,0:T(8,128)}, f32[2,128,128]{2,1,0:T(8,128)}) async-done(((f32[2,2,128,128]{3,2,1,0:T(8,128)}, f32[2,256,128]{2,1,0:T(8,128)}, f32[2,128,128]{2,1,0:T(8,128)}), (f32[2,2,128,128]{3,2,1,0:T(8,128)}, f32[2,256,128]{2,1,0:T(8,128)}, f32[2,128,128]{2,1,0:T(8,128)})) %all-reduce.49.cloned.1.call-update) | async-done | bytes 655376 | tf_op jit(solution)/shard_map/psum | solution.py:254
  532.9 1.7 broadcast_multiply_fusion.3
  534.5 1.6 broadcast_multiply_fusion.5
  536.1 1.7 broadcast_multiply_fusion.2
  (300 shorter events, 86.1 us)
Async XLA Ops:
  7.2 405.3 %all-reduce.51.cloned.1.call-start = ((), (), s32[]{:S(2)}) async-start(), calls=%async_computation.1 | async-start | bytes 1310720 | tf_op jit(solution)/shard_map/psum | solution.py:254
  8.9 6.6 %copy-start.15 = (bf16[2,7,2,8,2,8,128]{6,5,4,3,2,1,0:T(8,128)(2,1)}, bf16[2,7,2,8,2,8,128]{6,5,4,3,2,1,0:T(8,128)(2,1)S(1)}, u32[]{:S(2)}) copy-start(bf16[2,7,2,8,2,8,128]{6,5,4,3,2,1,0:T(8,128)(2,1)S(1)} %fusion.22) | copy-start | bytes 2752516
  8.9 1.6 copy-start
  10.5 1.8 copy-start.19
  10.5 1.2 copy-start.29
  10.5 1.8 copy-start.10
  12.3 7.7 %copy-start.30 = (f32[128]{0:T(128)}, f32[128]{0:T(128)S(1)}, u32[]{:S(2)}) copy-start(f32[128]{0:T(128)S(1)} %get-tuple-element.83) | copy-start | bytes 1540
  14.2 0.9 copy-start.21
  17.3 0.9 copy-start.17
  20.0 1.8 copy-start.13
  21.8 1.0 copy-start.8
  26.4 1.3 copy-start.1
  26.7 1.1 copy-start.5
  28.5 8.1 %collective-permute-start = (f32[1,16,2,8,128]{4,1,0,3,2:T(8,128)}, f32[1,16,2,8,128]{4,1,0,3,2:T(8,128)S(1)}, u32[]{:S(2)}, u32[]{:S(2)}) collective-permute-start(f32[1,16,2,8,128]{4,1,0,3,2:T(8,128)} %get-tuple-element.59), channel_id=1, source_target_pairs={{0,32},{32,64},{64,96},{96,128},{128,160},{160,192},{192,224},{1,3... | collective-permute-start | bytes 393224 | tf_op jit(solution)/shard_map/ppermute | solution.py:18
  32.9 6.7 %collective-permute-start.1 = (f32[1,16,2,8,128]{4,1,0,3,2:T(8,128)}, f32[1,16,2,8,128]{4,1,0,3,2:T(8,128)}, u32[]{:S(2)}, u32[]{:S(2)}) collective-permute-start(f32[1,16,2,8,128]{4,1,0,3,2:T(8,128)} %get-tuple-element.60), channel_id=1, source_target_pairs={{32,0},{64,32},{96,64},{128,96},{160,128},{192,160},{224,192},{33,... | collective-permute-start | bytes 393224 | tf_op jit(solution)/shard_map/ppermute | solution.py:20
  41.3 7.1 %collective-permute-start.2 = (f32[18,1,2,8,128]{4,1,0,3,2:T(1,128)}, f32[18,1,2,8,128]{4,1,0,3,2:T(1,128)S(1)}, u32[]{:S(2)}, u32[]{:S(2)}) collective-permute-start(f32[18,1,2,8,128]{4,1,0,3,2:T(1,128)} %get-tuple-element.33), channel_id=1, source_target_pairs={{0,8},{8,16},{16,24},{1,9},{9,17},{17,25},{2,10},{10,18},{18,26},{... | collective-permute-start | bytes 442376 | tf_op jit(solution)/shard_map/ppermute | solution.py:18
  46.1 6.8 %collective-permute-start.3 = (f32[18,1,2,8,128]{4,1,0,3,2:T(1,128)}, f32[18,1,2,8,128]{4,1,0,3,2:T(1,128)}, u32[]{:S(2)}, u32[]{:S(2)}) collective-permute-start(f32[18,1,2,8,128]{4,1,0,3,2:T(1,128)} %get-tuple-element.34), channel_id=1, source_target_pairs={{8,0},{16,8},{24,16},{9,1},{17,9},{25,17},{10,2},{18,10},{26,18},{... | collective-permute-start | bytes 442376 | tf_op jit(solution)/shard_map/ppermute | solution.py:20
  48.5 5.9 %copy-start.6 = (f32[18,1,2,8,128]{4,1,0,3,2:T(1,128)}, f32[18,1,2,8,128]{4,1,0,3,2:T(1,128)S(1)}, u32[]{:S(2)}) copy-start(f32[18,1,2,8,128]{4,1,0,3,2:T(1,128)S(1)} %collective-permute-done.2) | copy-start | bytes 442372
  54.5 1.0 copy-start.7
  57.5 5.1 collective-permute-start.4
  62.6 6.1 %collective-permute-start.5 = (f32[16,16,1,128]{3,1,0,2:T(8,128)S(1)}, f32[16,16,1,128]{3,1,0,2:T(8,128)S(1)}, u32[]{:S(2)}, u32[]{:S(2)}) collective-permute-start(f32[16,16,1,128]{3,1,0,2:T(8,128)S(1)} %get-tuple-element.79), channel_id=1, source_target_pairs={{1,0},{2,1},{3,2},{4,3},{5,4},{6,5},{7,6},{9,8},{10,9},{11,10},{12... | collective-permute-start | bytes 393224 | tf_op jit(solution)/shard_map/ppermute | solution.py:20
  69.7 1.8 copy-start.27
  69.7 1.8 copy-start.32
  71.4 2.1 copy-start.28
  74.6 0.9 copy-start.11
  74.7 0.9 copy-start.33
  87.4 6.2 %collective-permute-start.6 = (f32[1,16,2,8,128]{4,1,0,2,3:T(8,128)S(1)}, f32[1,16,2,8,128]{4,1,0,2,3:T(8,128)S(1)}, u32[]{:S(2)}, u32[]{:S(2)}) collective-permute-start(f32[1,16,2,8,128]{4,1,0,2,3:T(8,128)S(1)} %get-tuple-element.51), channel_id=1, source_target_pairs={{0,32},{32,64},{64,96},{96,128},{128,160},{160,192},{192,224},{1,3... | collective-permute-start | bytes 393224 | tf_op jit(solution)/shard_map/ppermute | solution.py:18
  90.9 7.8 %collective-permute-start.7 = (f32[1,16,2,8,128]{4,1,0,2,3:T(8,128)S(1)}, f32[1,16,2,8,128]{4,1,0,2,3:T(8,128)S(1)}, u32[]{:S(2)}, u32[]{:S(2)}) collective-permute-start(f32[1,16,2,8,128]{4,1,0,2,3:T(8,128)S(1)} %get-tuple-element.52), channel_id=1, source_target_pairs={{32,0},{64,32},{96,64},{128,96},{160,128},{192,160},{224,192},{33,... | collective-permute-start | bytes 393224 | tf_op jit(solution)/shard_map/ppermute | solution.py:20
  99.0 6.3 %collective-permute-start.8 = (f32[18,1,2,8,128]{4,1,0,2,3:T(1,128)S(1)}, f32[18,1,2,8,128]{4,1,0,2,3:T(1,128)S(1)}, u32[]{:S(2)}, u32[]{:S(2)}) collective-permute-start(f32[18,1,2,8,128]{4,1,0,2,3:T(1,128)S(1)} %get-tuple-element.31), channel_id=1, source_target_pairs={{0,8},{8,16},{16,24},{1,9},{9,17},{17,25},{2,10},{10,18},{18,26},{... | collective-permute-start | bytes 442376 | tf_op jit(solution)/shard_map/ppermute | solution.py:18
  103.2 6.5 %collective-permute-start.9 = (f32[18,1,2,8,128]{4,1,0,2,3:T(1,128)S(1)}, f32[18,1,2,8,128]{4,1,0,2,3:T(1,128)S(1)}, u32[]{:S(2)}, u32[]{:S(2)}) collective-permute-start(f32[18,1,2,8,128]{4,1,0,2,3:T(1,128)S(1)} %get-tuple-element.32), channel_id=1, source_target_pairs={{8,0},{16,8},{24,16},{9,1},{17,9},{25,17},{10,2},{18,10},{26,18},{... | collective-permute-start | bytes 442376 | tf_op jit(solution)/shard_map/ppermute | solution.py:20
  111.5 5.6 %collective-permute-start.10 = (f32[16,16,1,128]{3,1,0,2:T(8,128)S(1)}, f32[16,16,1,128]{3,1,0,2:T(8,128)S(1)}, u32[]{:S(2)}, u32[]{:S(2)}) collective-permute-start(f32[16,16,1,128]{3,1,0,2:T(8,128)S(1)} %dynamic-slice_bitcast_fusion.2), channel_id=1, source_target_pairs={{0,1},{1,2},{2,3},{3,4},{4,5},{5,6},{6,7},{8,9},{9,10},{10,11},{11... | collective-permute-start | bytes 393224 | tf_op jit(solution)/shard_map/ppermute | solution.py:18
  117.8 6.1 %collective-permute-start.11 = (f32[16,16,1,128]{3,2,1,0:T(1,128)S(1)}, f32[16,16,1,128]{3,2,1,0:T(1,128)S(1)}, u32[]{:S(2)}, u32[]{:S(2)}) collective-permute-start(f32[16,16,1,128]{3,2,1,0:T(1,128)S(1)} %get-tuple-element.77), channel_id=1, source_target_pairs={{1,0},{2,1},{3,2},{4,3},{5,4},{6,5},{7,6},{9,8},{10,9},{11,10},{12... | collective-permute-start | bytes 393224 | tf_op jit(solution)/shard_map/ppermute | solution.py:20
  125.4 1.2 copy-start.12
  125.4 1.2 copy-start.34
  132.5 7.2 %collective-permute-start.12 = (f32[1,16,2,8,128]{4,1,0,3,2:T(8,128)S(1)}, f32[1,16,2,8,128]{4,1,0,3,2:T(8,128)S(1)}, u32[]{:S(2)}, u32[]{:S(2)}) collective-permute-start(f32[1,16,2,8,128]{4,1,0,3,2:T(8,128)S(1)} %get-tuple-element.43), channel_id=1, source_target_pairs={{0,32},{32,64},{64,96},{96,128},{128,160},{160,192},{192,224},{1,3... | collective-permute-start | bytes 393224 | tf_op jit(solution)/shard_map/ppermute | solution.py:18
  137.1 6.7 %collective-permute-start.13 = (f32[1,16,2,8,128]{4,1,0,3,2:T(8,128)S(1)}, f32[1,16,2,8,128]{4,1,0,3,2:T(8,128)S(1)}, u32[]{:S(2)}, u32[]{:S(2)}) collective-permute-start(f32[1,16,2,8,128]{4,1,0,3,2:T(8,128)S(1)} %get-tuple-element.44), channel_id=1, source_target_pairs={{32,0},{64,32},{96,64},{128,96},{160,128},{192,160},{224,192},{33,... | collective-permute-start | bytes 393224 | tf_op jit(solution)/shard_map/ppermute | solution.py:20
  144.0 7.1 %collective-permute-start.14 = (f32[18,1,2,8,128]{4,1,0,3,2:T(1,128)S(1)}, f32[18,1,2,8,128]{4,1,0,3,2:T(1,128)S(1)}, u32[]{:S(2)}, u32[]{:S(2)}) collective-permute-start(f32[18,1,2,8,128]{4,1,0,3,2:T(1,128)S(1)} %get-tuple-element.27), channel_id=1, source_target_pairs={{0,8},{8,16},{16,24},{1,9},{9,17},{17,25},{2,10},{10,18},{18,26},{... | collective-permute-start | bytes 442376 | tf_op jit(solution)/shard_map/ppermute | solution.py:18
  148.3 6.5 %collective-permute-start.15 = (f32[18,1,2,8,128]{4,1,0,3,2:T(1,128)S(1)}, f32[18,1,2,8,128]{4,1,0,3,2:T(1,128)S(1)}, u32[]{:S(2)}, u32[]{:S(2)}) collective-permute-start(f32[18,1,2,8,128]{4,1,0,3,2:T(1,128)S(1)} %get-tuple-element.28), channel_id=1, source_target_pairs={{8,0},{16,8},{24,16},{9,1},{17,9},{25,17},{10,2},{18,10},{26,18},{... | collective-permute-start | bytes 442376 | tf_op jit(solution)/shard_map/ppermute | solution.py:20
  156.5 7.6 %collective-permute-start.16 = (f32[16,16,1,128]{3,1,0,2:T(8,128)S(1)}, f32[16,16,1,128]{3,1,0,2:T(8,128)S(1)}, u32[]{:S(2)}, u32[]{:S(2)}) collective-permute-start(f32[16,16,1,128]{3,1,0,2:T(8,128)S(1)} %dynamic-slice_bitcast_fusion.1), channel_id=1, source_target_pairs={{0,1},{1,2},{2,3},{3,4},{4,5},{5,6},{6,7},{8,9},{9,10},{10,11},{11... | collective-permute-start | bytes 393224 | tf_op jit(solution)/shard_map/ppermute | solution.py:18
  164.2 6.4 %collective-permute-start.17 = (f32[16,16,1,128]{3,1,0,2:T(8,128)S(1)}, f32[16,16,1,128]{3,1,0,2:T(8,128)S(1)}, u32[]{:S(2)}, u32[]{:S(2)}) collective-permute-start(f32[16,16,1,128]{3,1,0,2:T(8,128)S(1)} %get-tuple-element.73), channel_id=1, source_target_pairs={{1,0},{2,1},{3,2},{4,3},{5,4},{6,5},{7,6},{9,8},{10,9},{11,10},{12... | collective-permute-start | bytes 393224 | tf_op jit(solution)/shard_map/ppermute | solution.py:20
  179.5 1.0 copy-start.3
  179.5 2.0 copy-start.38
  184.4 2.0 copy-start.2
  189.5 6.6 %collective-permute-start.18 = (f32[1,16,2,8,128]{4,1,0,3,2:T(8,128)S(1)}, f32[1,16,2,8,128]{4,1,0,3,2:T(8,128)S(1)}, u32[]{:S(2)}, u32[]{:S(2)}) collective-permute-start(f32[1,16,2,8,128]{4,1,0,3,2:T(8,128)S(1)} %get-tuple-element.35), channel_id=1, source_target_pairs={{0,32},{32,64},{64,96},{96,128},{128,160},{160,192},{192,224},{1,3... | collective-permute-start | bytes 393224 | tf_op jit(solution)/shard_map/ppermute | solution.py:18
  193.1 6.4 %collective-permute-start.19 = (f32[1,16,2,8,128]{4,1,0,3,2:T(8,128)S(1)}, f32[1,16,2,8,128]{4,1,0,3,2:T(8,128)S(1)}, u32[]{:S(2)}, u32[]{:S(2)}) collective-permute-start(f32[1,16,2,8,128]{4,1,0,3,2:T(8,128)S(1)} %get-tuple-element.36), channel_id=1, source_target_pairs={{32,0},{64,32},{96,64},{128,96},{160,128},{192,160},{224,192},{33,... | collective-permute-start | bytes 393224 | tf_op jit(solution)/shard_map/ppermute | solution.py:20
  199.7 6.9 %collective-permute-start.20 = (f32[18,1,2,8,128]{4,1,0,3,2:T(1,128)S(1)}, f32[18,1,2,8,128]{4,1,0,3,2:T(1,128)S(1)}, u32[]{:S(2)}, u32[]{:S(2)}) collective-permute-start(f32[18,1,2,8,128]{4,1,0,3,2:T(1,128)S(1)} %get-tuple-element.25), channel_id=1, source_target_pairs={{0,8},{8,16},{16,24},{1,9},{9,17},{17,25},{2,10},{10,18},{18,26},{... | collective-permute-start | bytes 442376 | tf_op jit(solution)/shard_map/ppermute | solution.py:18
  204.0 6.5 %collective-permute-start.21 = (f32[18,1,2,8,128]{4,1,0,3,2:T(1,128)S(1)}, f32[18,1,2,8,128]{4,1,0,3,2:T(1,128)S(1)}, u32[]{:S(2)}, u32[]{:S(2)}) collective-permute-start(f32[18,1,2,8,128]{4,1,0,3,2:T(1,128)S(1)} %get-tuple-element.26), channel_id=1, source_target_pairs={{8,0},{16,8},{24,16},{9,1},{17,9},{25,17},{10,2},{18,10},{26,18},{... | collective-permute-start | bytes 442376 | tf_op jit(solution)/shard_map/ppermute | solution.py:20
  212.3 9.2 %collective-permute-start.22 = (f32[16,16,1,128]{3,1,0,2:T(8,128)S(1)}, f32[16,16,1,128]{3,1,0,2:T(8,128)S(1)}, u32[]{:S(2)}, u32[]{:S(2)}) collective-permute-start(f32[16,16,1,128]{3,1,0,2:T(8,128)S(1)} %dynamic-slice_bitcast_fusion), channel_id=1, source_target_pairs={{0,1},{1,2},{2,3},{3,4},{4,5},{5,6},{6,7},{8,9},{9,10},{10,11},{11... | collective-permute-start | bytes 393224 | tf_op jit(solution)/shard_map/ppermute | solution.py:18
  221.6 6.4 %collective-permute-start.23 = (f32[16,16,1,128]{3,1,0,2:T(8,128)S(1)}, f32[16,16,1,128]{3,1,0,2:T(8,128)S(1)}, u32[]{:S(2)}, u32[]{:S(2)}) collective-permute-start(f32[16,16,1,128]{3,1,0,2:T(8,128)S(1)} %get-tuple-element.71), channel_id=1, source_target_pairs={{1,0},{2,1},{3,2},{4,3},{5,4},{6,5},{7,6},{9,8},{10,9},{11,10},{12... | collective-permute-start | bytes 393224 | tf_op jit(solution)/shard_map/ppermute | solution.py:20
  229.3 9.5 %copy-start.23 = (bf16[2,7,2,8,2,8,128]{6,5,4,3,2,1,0:T(8,128)(2,1)}, bf16[2,7,2,8,2,8,128]{6,5,4,3,2,1,0:T(8,128)(2,1)S(1)}, u32[]{:S(2)}) copy-start(bf16[2,7,2,8,2,8,128]{6,5,4,3,2,1,0:T(8,128)(2,1)S(1)} %fusion.16) | copy-start | bytes 2752516
  229.5 1.3 copy-start.9
  230.8 1.5 copy-start.37
  232.3 1.2 copy-start.14
  234.0 1.8 copy-start.22
  235.7 1.5 copy-start.36
  237.2 1.2 copy-start.20
  238.4 1.5 copy-start.35
  240.8 94.0 %copy-start.25 = (bf16[2,7,2,8,2,8,128]{6,5,4,3,2,1,0:T(8,128)(2,1)}, bf16[2,7,2,8,2,8,128]{6,5,4,3,2,1,0:T(8,128)(2,1)S(1)}, u32[]{:S(2)}) copy-start(bf16[2,7,2,8,2,8,128]{6,5,4,3,2,1,0:T(8,128)(2,1)S(1)} %get-tuple-element.112) | copy-start | bytes 2752516
  240.8 95.7 %copy-start.18 = (bf16[2,7,2,8,2,8,128]{6,5,4,3,2,1,0:T(8,128)(2,1)S(1)}, bf16[2,7,2,8,2,8,128]{6,5,4,3,2,1,0:T(8,128)(2,1)}, u32[]{:S(2)}) copy-start(bf16[2,7,2,8,2,8,128]{6,5,4,3,2,1,0:T(8,128)(2,1)} %copy-done.17) | copy-start | bytes 2752516
  334.8 1.7 copy-start.24
  336.5 1.2 copy-start.16
  336.5 1.5 copy-start.26
  339.2 193.6 %all-reduce.49.cloned.1.call-start = ((), (), s32[]{:S(2)}) async-start(), calls=%async_computation | async-start | bytes 1310720 | tf_op jit(solution)/shard_map/psum | solution.py:254
  339.7 72.8 %copy-start.4 = (bf16[16,16,2,8,128]{4,3,2,1,0:T(8,128)(2,1)S(1)}, bf16[16,16,2,8,128]{4,3,2,1,0:T(8,128)(2,1)}, u32[]{:S(2)}) copy-start(bf16[16,16,2,8,128]{4,3,2,1,0:T(8,128)(2,1)} %copy-done.3) | copy-start | bytes 3145732
  (1 other events, 0.7 us)
Sparse Core Ops, SparseCore 0:
  339.3 73.0 all-reduce.50
  416.0 116.8 all-reduce.48
